TPU v7x, 32 devices: a whole 2x2x4 slice. The times are simulated.
32 devices in a mesh: dp: 8 (over y, x, core), mp: 4 (over z).
Axes of the slice: x: 2, y: 2, z: 4, core: 2. Of those that a mesh axis runs over, the one named last changes fastest.
Arguments:
- states: bfloat16 [512, 64, 256], P('dp', 'mp'), may hold values from -6 to 6
- key_embed: bfloat16 [512, 128], P('dp'), may hold values from -6 to 6
- partner: int32 [512], replicated, may hold values from 0 to 511, as said below
- mix_numer: int32 [512], P('dp'), may hold values from 1 to 15
- lengths: int32 [512], replicated, may hold values from 8 to 64
- w_qkv: bfloat16 [3, 256, 256], P(None, None, 'mp'), may hold values from -0.375 to 0.375
- w_out: bfloat16 [256, 256], P('mp'), may hold values from -0.375 to 0.375
- w_up: bfloat16 [256, 1024], P(None, 'mp'), may hold values from -0.375 to 0.375
- w_down: bfloat16 [1024, 256], P('mp'), may hold values from -0.1875 to 0.1875
- w_proj: bfloat16 [256, 128], replicated, may hold values from -0.375 to 0.375
Outputs:
- session_loss: float32 [512], P('dp')
- grad_states: float32 [512, 64, 256], P('dp', 'mp')
Inputs may be any that keep to these rules, and one draw needn't show every extreme that they name: partner is a permutation of the 512 sessions; a session and its partner lie in different aligned blocks of 64 sessions, and at most 10 sessions of one block have their partners in one same other block.
All inputs are finite; a program needn't handle non-finite values.
Results may differ from a plain program's by a relative error of at most 0.0091.
Values may be sent and summed in bfloat16 or wider, within the bound.
A program may use at most 64 MiB of HBM per device.

v0:
```python
import jax
import jax.numpy as jnp
from jax import lax
from jax.sharding import PartitionSpec as P

HD = 64
SOFTMAX_TEMP = 0.1
LN_EPS = 1e-05
NORM_EPS = 1e-06
TOP_PRECISION = lax.Precision.HIGHEST


def swap_rows(buffer):
    return lax.all_to_all(buffer, "dp", split_axis=0, concat_axis=0, tiled=True)


def local(states, key_embed, partner, mix_numer, lengths, w_qkv, w_out, w_up, w_down, w_proj):
    sessions_dev, ev_part, width = states.shape
    n_data = lax.axis_size("dp")
    capacity = (sessions_dev + n_data - 2) // (n_data - 1)
    device_index = lax.axis_index("dp")
    model_index = lax.axis_index("mp")
    all_keys = lax.all_gather(key_embed, "dp", axis=0, tiled=True)
    session_count = partner.shape[0]
    local_ids = jnp.arange(sessions_dev, dtype=jnp.int32)
    own_ids = device_index * sessions_dev + local_ids
    own_partner = lax.dynamic_slice_in_dim(partner, device_index * sessions_dev, sessions_dev)
    mixup_weight = mix_numer.astype(jnp.float32) / 16.0
    source = own_partner // sessions_dev
    earlier = local_ids[None, :] < local_ids[:, None]
    in_slot = jnp.sum(((source[:, None] == source[None, :]) & earlier).astype(jnp.int32), axis=1)
    wanted = partner[None, :] == own_ids[:, None]
    seeker = jnp.sum(
        jnp.where(wanted, jnp.arange(session_count, dtype=jnp.int32)[None, :], 0), axis=1
    )
    target = seeker // sessions_dev
    seeker_rows = partner.reshape(n_data, sessions_dev)[target]
    out_slot = jnp.sum(
        (
            (seeker_rows // sessions_dev == device_index)
            & (local_ids[None, :] < (seeker % sessions_dev)[:, None])
        ).astype(jnp.int32),
        axis=1,
    )
    row_len = ev_part * width
    outgoing = (
        jnp.zeros((n_data, capacity, row_len), jnp.bfloat16)
        .at[target, out_slot]
        .set(states.reshape(sessions_dev, row_len))
    )
    incoming = swap_rows(outgoing)
    partner_states = incoming[source, in_slot].reshape(sessions_dev, ev_part, width)
    mix_rows = mixup_weight[:, None, None]
    mixed_part = (
        mix_rows * states.astype(jnp.float32)
        + (1.0 - mix_rows) * partner_states.astype(jnp.float32)
    ).astype(jnp.bfloat16)
    own_lengths = lax.dynamic_slice_in_dim(lengths, device_index * sessions_dev, sessions_dev)
    len_mix = jnp.maximum(own_lengths, lengths[own_partner])
    qkv_full, out_full, up_full, down_full = (w_qkv, w_out, w_up, w_down)
    mixed = lax.all_gather(mixed_part, "mp", axis=1, tiled=True)
    layer_sessions = mixed.shape[0]
    events = mixed.shape[1]
    rows = layer_sessions * events
    positions = jnp.arange(events, dtype=jnp.int32)
    token_mask = (positions[None, :] < len_mix[:, None]).astype(jnp.float32)
    pool_weights = token_mask / len_mix[:, None].astype(jnp.float32)
    inputs_f = mixed.astype(jnp.float32).reshape(rows, width)
    row_mean = jnp.mean(inputs_f, axis=1, keepdims=True)
    centered = inputs_f - row_mean
    inv_std = lax.rsqrt(jnp.mean(centered * centered, axis=1, keepdims=True) + LN_EPS)
    unit_rows = centered * inv_std
    normed = unit_rows.astype(jnp.bfloat16)
    projected = jnp.einsum(
        "rd,jdf->jrf", normed, qkv_full, preferred_element_type=jnp.float32
    ).astype(jnp.bfloat16)
    inner_part = qkv_full.shape[2]
    heads_part = inner_part // HD
    query_h = projected[0].reshape(layer_sessions, events, heads_part, HD)
    key_h = projected[1].reshape(layer_sessions, events, heads_part, HD)
    value_h = projected[2].reshape(layer_sessions, events, heads_part, HD)
    score_scale = HD ** (-0.5)
    scores = (
        jnp.einsum("sthc,srhc->shtr", query_h, key_h, preferred_element_type=jnp.float32)
        * score_scale
    )
    exp_scores = jnp.exp(scores) * token_mask[:, None, None, :]
    probs = exp_scores / jnp.sum(exp_scores, axis=3, keepdims=True)
    probs_b = probs.astype(jnp.bfloat16)
    context = (
        jnp.einsum("shtr,srhc->sthc", probs_b, value_h, preferred_element_type=jnp.float32)
        .astype(jnp.bfloat16)
        .reshape(rows, inner_part)
    )
    pre_act = jnp.dot(normed, up_full, preferred_element_type=jnp.float32)
    hidden = jax.nn.gelu(pre_act).astype(jnp.bfloat16)
    branch = jnp.dot(context, out_full, preferred_element_type=jnp.float32) + jnp.dot(
        hidden, down_full, preferred_element_type=jnp.float32
    )
    pooled_branch = jnp.einsum(
        "st,std->sd",
        pool_weights,
        branch.reshape(layer_sessions, events, width),
        precision=TOP_PRECISION,
    )
    pooled_input = jnp.einsum(
        "st,std->sd",
        pool_weights,
        inputs_f.reshape(layer_sessions, events, width),
        precision=TOP_PRECISION,
    )
    pooled = lax.psum(pooled_branch, "mp") + pooled_input
    proj_f = w_proj.astype(jnp.float32)
    embed = jnp.dot(pooled, proj_f, precision=TOP_PRECISION)
    inv_norm = lax.rsqrt(jnp.sum(embed * embed, axis=1, keepdims=True) + NORM_EPS)
    unit_query_rows = embed * inv_norm
    keys_f = all_keys.astype(jnp.float32)
    unit_key_rows = keys_f * lax.rsqrt(jnp.sum(keys_f * keys_f, axis=1, keepdims=True) + NORM_EPS)
    pair_logits = (
        jnp.einsum("an,qn->aq", unit_query_rows, unit_key_rows, precision=TOP_PRECISION)
        / SOFTMAX_TEMP
    )
    exp_logits = jnp.exp(pair_logits)
    sum_exp = jnp.sum(exp_logits, axis=1)
    own_logit = jnp.take_along_axis(pair_logits, own_ids[:, None], axis=1)[:, 0]
    partner_logit = jnp.take_along_axis(pair_logits, own_partner[:, None], axis=1)[:, 0]
    session_loss = (
        jnp.log(sum_exp) - mixup_weight * own_logit - (1.0 - mixup_weight) * partner_logit
    )
    normalized_exponent = exp_logits / sum_exp[:, None]
    unit_gradient = (
        jnp.dot(normalized_exponent, unit_key_rows, precision=TOP_PRECISION)
        - mixup_weight[:, None] * unit_key_rows[own_ids]
        - (1.0 - mixup_weight)[:, None] * unit_key_rows[own_partner]
    ) / SOFTMAX_TEMP
    grad_embed = (
        unit_gradient
        - unit_query_rows * jnp.sum(unit_query_rows * unit_gradient, axis=1, keepdims=True)
    ) * inv_norm
    grad_pooled = jnp.einsum("se,de->sd", grad_embed, proj_f, precision=TOP_PRECISION)
    grad_full = grad_pooled[:, None, :] * pool_weights[:, :, None]
    grad_b = grad_full.reshape(rows, width).astype(jnp.bfloat16)
    d_hidden = jnp.einsum("rd,fd->rf", grad_b, down_full, preferred_element_type=jnp.float32)
    d_pre = jax.vjp(jax.nn.gelu, pre_act)[1](d_hidden)[0].astype(jnp.bfloat16)
    d_context = (
        jnp.einsum("rd,fd->rf", grad_b, out_full, preferred_element_type=jnp.float32)
        .astype(jnp.bfloat16)
        .reshape(layer_sessions, events, heads_part, HD)
    )
    d_value = jnp.einsum(
        "shtr,sthc->srhc", probs_b, d_context, preferred_element_type=jnp.float32
    ).astype(jnp.bfloat16)
    d_prob = jnp.einsum("sthc,srhc->shtr", d_context, value_h, preferred_element_type=jnp.float32)
    d_score = (
        probs * (d_prob - jnp.sum(probs * d_prob, axis=3, keepdims=True)) * score_scale
    ).astype(jnp.bfloat16)
    d_query = jnp.einsum(
        "shtr,srhc->sthc", d_score, key_h, preferred_element_type=jnp.float32
    ).astype(jnp.bfloat16)
    d_key = jnp.einsum(
        "shtr,sthc->srhc", d_score, query_h, preferred_element_type=jnp.float32
    ).astype(jnp.bfloat16)
    d_proj = jnp.stack([d_query, d_key, d_value]).reshape(3, rows, inner_part)
    d_normed = jnp.einsum(
        "jrf,jdf->rd", d_proj, qkv_full, preferred_element_type=jnp.float32
    ) + jnp.einsum("rf,df->rd", d_pre, up_full, preferred_element_type=jnp.float32)
    d_normed = d_normed.reshape(layer_sessions, events, width)
    unit_all = unit_rows.reshape(layer_sessions, events, width)
    inv_all = inv_std.reshape(layer_sessions, events, 1)
    event_start = model_index * ev_part
    unit_part = lax.dynamic_slice_in_dim(unit_all, event_start, ev_part, 1)
    inv_part = lax.dynamic_slice_in_dim(inv_all, event_start, ev_part, 1)
    d_full = lax.psum(d_normed, "mp")
    d_local = lax.dynamic_slice_in_dim(d_full, event_start, ev_part, 1)
    center = jnp.mean(d_local, axis=2, keepdims=True)
    along = jnp.mean(d_local * unit_part, axis=2, keepdims=True)
    d_mixed = (
        lax.dynamic_slice_in_dim(grad_full, event_start, ev_part, 1)
        + (d_local - center - unit_part * along) * inv_part
    )
    d_mixed_rows = d_mixed.reshape(sessions_dev, row_len)
    back_rows = ((1.0 - mixup_weight)[:, None] * d_mixed_rows).astype(jnp.bfloat16)
    returning = (
        jnp.zeros((n_data, capacity, row_len), jnp.bfloat16).at[source, in_slot].set(back_rows)
    )
    arrived = swap_rows(returning)
    grad_states = mixup_weight[:, None] * d_mixed_rows + arrived[target, out_slot].astype(
        jnp.float32
    )
    return (session_loss, grad_states.reshape(sessions_dev, ev_part, width))


def solution(mesh):
    placed = (
        P("dp", "mp", None),
        P("dp", None),
        P(),
        P("dp"),
        P(),
        P(None, None, "mp"),
        P("mp", None),
        P(None, "mp"),
        P("mp", None),
        P(),
    )
    return jax.shard_map(
        local, mesh=mesh, in_specs=placed, out_specs=(P("dp"), P("dp", "mp", None)), check_vma=False
    )
```

profile of v0, /device:TPU:0, one launch (start us, length us, event | category | flops | bytes accessed | tf_op | source)
XLA Modules:
  0.0 415.0 jit_solution(1312834488764694528)
XLA Ops:
  12.3 9.7 %scatter_fusion = bf16[8,10,4096]{2,0,1:T(8,128)(2,1)S(1)} fusion(bf16[8,10,4096]{2,0,1:T(8,128)(2,1)S(1)} %broadcast.348.clone, s32[64]{0:T(128)S(1)} %get-tuple-element.15, bf16[64,4096]{1,0:T(8,128)(2,1)S(1)} %bitcast.216), kind=kCustom, calls=%fused_computation.8 | custom fusion | bytes 1573376 | tf_op jit(solution)/shard_map/scatter | solution.py:49
  23.4 5.2 %all-to-all-start = ((bf16[8,10,4096]{2,1,0:T(8,128)(2,1)}), bf16[8,10,4096]{2,1,0:T(8,128)(2,1)S(1)}, u32[]{:S(2)}, u32[]{:S(2)}) async-start(bf16[8,10,4096]{2,1,0:T(8,128)(2,1)} %copy.60), calls=%async_computation | async-start | bytes 2097152 | tf_op jit(solution)/shard_map/all_to_all | solution.py:14
  28.8 15.1 %all-to-all-done = bf16[8,10,4096]{2,1,0:T(8,128)(2,1)S(1)} async-done(((bf16[8,10,4096]{2,1,0:T(8,128)(2,1)}), bf16[8,10,4096]{2,1,0:T(8,128)(2,1)S(1)}, u32[]{:S(2)}, u32[]{:S(2)}) %all-to-all-start) | async-done | bytes 655392 | tf_op jit(solution)/shard_map/all_to_all | solution.py:14
  44.3 2.2 gather_fusion.2
  49.5 8.2 %all_gather.7 = bf16[512,128]{1,0:T(8,128)(2,1)S(1)} all-gather(bf16[64,128]{1,0:T(8,128)(2,1)S(1)} %copy-done.17), channel_id=1, replica_groups=mesh['dp'=8,'mp'=4] {'dp'}, dimensions={0}, use_global_device_ids=true | all-gather | bytes 147456 | tf_op jit(solution)/shard_map/all_gather | solution.py:23
  61.1 31.9 %all-gather.2.cloned.1.call-done = bf16[64,64,256]{2,1,0:T(8,128)(2,1)} async-done(((bf16[64,16,256]{2,1,0:T(8,128)(2,1)}), bf16[64,64,256]{2,1,0:T(8,128)(2,1)}) %all-gather.2.cloned.1.call-update) | async-done | bytes 2097168 | tf_op jit(solution)/shard_map/all_gather | solution.py:61
  93.0 2.4 convert_reduce_fusion
  95.4 3.1 broadcast_subtract_fusion
  98.6 2.5 fusion.10
  108.9 3.7 fusion.132
  112.6 5.0 %fusion.26 = (f32[64,64]{1,0:T(8,128)S(1)}, f32[64,64,64]{1,2,0:T(8,128)S(1)}) fusion(f32[64,64]{1,0:T(8,128)S(1)} %copy-done.15, bf16[64,64,64]{1,0,2:T(8,128)(2,1)S(1)} %copy-done.9, bf16[64,64,64]{1,0,2:T(8,128)(2,1)S(1)} %copy-done.7), kind=kOutput, calls=%fused_computation.48 | convolution fusion | flops 34336768 | bytes 2129920 | tf_op jit(solution)/shard_map/sthc,srhc->shtr/dot_general | solution.py:84
  129.2 31.5 %all-reduce.3.cloned.1.call-done = f32[64,256]{1,0:T(8,128)} async-done(((f32[64,256]{1,0:T(8,128)}), f32[64,256]{1,0:T(8,128)}) %all-reduce.3.cloned.1.call-update) | async-done | bytes 65552 | tf_op jit(solution)/shard_map/psum | solution.py:112
  167.9 2.8 reshape.407
  170.7 3.8 fusion.58
  174.5 3.4 fusion.45
  177.8 6.9 %fusion.49 = bf16[64,64,1,64]{1,3,0,2:T(8,128)(2,1)} fusion(f32[64,64,64]{1,2,0:T(8,128)} %fusion.58, bf16[64,64,64]{1,0,2:T(8,128)(2,1)} %reshape.404, f32[64,64,64]{1,2,0:T(8,128)} %copy-done.27, f32[64,64]{1,0:T(8,128)} %copy-done.29, f32[64,64]{1,0:T(8,128)} %fusion.80), kind=kOutput, calls=%fused_computation.64 | convolution fusion | flops 36704320 | bytes 3178496 | tf_op jit(solution)/shard_map/shtr,srhc->sthc/dot_general | solution.py:157
  184.7 7.8 %fusion.46 = bf16[64,64,1,64]{1,3,0,2:T(8,128)(2,1)} fusion(f32[64,64,64]{1,2,0:T(8,128)} %fusion.58, bf16[64,64,64]{1,0,2:T(8,128)(2,1)S(1)} %copy-done.8, f32[64,64,64]{1,2,0:T(8,128)} %copy-done.27, f32[64,64]{1,0:T(8,128)} %copy-done.29, f32[64,64]{1,0:T(8,128)} %fusion.80), kind=kOutput, calls=%fused_computation.63 | convolution fusion | flops 36704320 | bytes 3178496 | tf_op jit(solution)/shard_map/shtr,sthc->srhc/dot_general | solution.py:160
  203.1 4.1 convolution_bitcast_fusion
  207.3 7.0 %convolution_add_fusion = f32[4096,256]{1,0:T(8,128)} fusion(f32[4096,256]{1,0:T(8,128)} %convolution_bitcast_fusion, bf16[256,256]{1,0:T(8,128)(2,1)S(1)} %copy-done.11, f32[4096,256]{1,0:T(8,128)} %fusion.132, bf16[4096,256]{1,0:T(8,128)(2,1)S(1)} %fusion.8, bf16[256,256]{1,0:T(8,128)(2,1)S(1)} %copy-done), kind=kOutput, calls=%fused_computation.13 | convolution fusion | flops 1095761920 | bytes 14942208 | tf_op jit(solution)/shard_map/rf,df->rd/dot_general | solution.py:166
  214.4 154.6 %all-reduce.5.cloned.1.call-done = f32[64,64,256]{2,1,0:T(8,128)} async-done(((f32[64,64,256]{2,1,0:T(8,128)}), f32[64,64,256]{2,1,0:T(8,128)}) %all-reduce.5.cloned.1.call-update) | async-done | bytes 4194320 | tf_op jit(solution)/shard_map/psum | solution.py:173
  374.0 9.7 %scatter_fusion.1 = bf16[8,10,4096]{2,0,1:T(8,128)(2,1)S(1)} fusion(bf16[8,10,4096]{2,0,1:T(8,128)(2,1)S(1)} %broadcast.348, s32[64]{0:T(128)S(1)} %get-tuple-element.16, bf16[64,4096]{1,0:T(8,128)(2,1)S(1)} %multiply_convert_fusion.3), kind=kCustom, calls=%fused_computation.9 | custom fusion | bytes 1573376 | tf_op jit(solution)/shard_map/scatter | solution.py:184
  385.1 3.9 all-to-all-start.1
  391.4 13.0 %all-to-all-done.1 = bf16[8,10,4096]{2,1,0:T(8,128)(2,1)S(1)} async-done(((bf16[8,10,4096]{2,1,0:T(8,128)(2,1)}), bf16[8,10,4096]{2,1,0:T(8,128)(2,1)S(1)}, u32[]{:S(2)}, u32[]{:S(2)}) %all-to-all-start.1) | async-done | bytes 655392 | tf_op jit(solution)/shard_map/all_to_all | solution.py:14
  404.7 2.2 gather_fusion.5
  (151 shorter events, 60.7 us)
Async XLA Ops:
  7.2 114.1 %copy-start = (bf16[256,256]{1,0:T(8,128)(2,1)S(1)}, bf16[256,256]{1,0:T(8,128)(2,1)}, u32[]{:S(2)}) copy-start(bf16[256,256]{1,0:T(8,128)(2,1)} %param.20) | copy-start | bytes 393220
  22.0 6.8 %copy-start.25 = (s32[64]{0:T(128)S(1)}, s32[64]{0:T(128)}, u32[]{:S(2)}) copy-start(s32[64]{0:T(128)} %param.15) | copy-start | bytes 772
  23.4 20.6 %all-to-all-start = ((bf16[8,10,4096]{2,1,0:T(8,128)(2,1)}), bf16[8,10,4096]{2,1,0:T(8,128)(2,1)S(1)}, u32[]{:S(2)}, u32[]{:S(2)}) async-start(bf16[8,10,4096]{2,1,0:T(8,128)(2,1)} %copy.60), calls=%async_computation | async-start | bytes 2097152 | tf_op jit(solution)/shard_map/all_to_all | solution.py:14
  28.6 64.4 %all-gather.2.cloned.1.call-start = ((), (), s32[]{:S(2)}) async-start(), calls=%async_computation.2 | async-start | bytes 2621440 | tf_op jit(solution)/shard_map/all_gather | solution.py:61
  28.8 17.9 %copy-start.21 = (f32[64]{0:T(128)}, f32[64]{0:T(128)S(1)}, u32[]{:S(2)}) copy-start(f32[64]{0:T(128)S(1)} %get-tuple-element.21) | copy-start | bytes 772
  28.8 17.9 %copy-start.23 = (f32[64]{0:T(128)}, f32[64]{0:T(128)S(1)}, u32[]{:S(2)}) copy-start(f32[64]{0:T(128)S(1)} %get-tuple-element.20) | copy-start | bytes 772
  47.8 112.9 %all-reduce.3.cloned.1.call-start = ((), (), s32[]{:S(2)}) async-start(), calls=%async_computation.3 | async-start | bytes 131072 | tf_op jit(solution)/shard_map/psum | solution.py:112
  108.8 3.8 copy-start.7
  108.8 3.8 copy-start.9
  108.8 3.8 copy-start.15
  124.7 3.0 copy-start.3
  127.4 33.3 %copy-start.10 = (bf16[256,128]{1,0:T(8,128)(2,1)S(1)}, bf16[256,128]{1,0:T(8,128)(2,1)}, u32[]{:S(2)}) copy-start(bf16[256,128]{1,0:T(8,128)(2,1)} %param.21) | copy-start | bytes 196612
  127.4 241.6 %all-reduce.5.cloned.1.call-start = ((), (), s32[]{:S(2)}) async-start(), calls=%async_computation.4 | async-start | bytes 8388608 | tf_op jit(solution)/shard_map/psum | solution.py:173
  160.7 5.6 %copy-start.13 = (bf16[64,256]{1,0:T(8,128)(2,1)S(1)}, bf16[64,256]{1,0:T(8,128)(2,1)}, u32[]{:S(2)}) copy-start(bf16[64,256]{1,0:T(8,128)(2,1)} %param.18) | copy-start | bytes 98308
  170.7 3.8 copy-start.5
  170.7 3.8 copy-start.16
  170.7 3.8 copy-start.28
  170.7 3.8 copy-start.30
  177.8 6.9 %copy-start.8 = (bf16[64,64,64]{1,0,2:T(8,128)(2,1)S(1)}, bf16[64,64,64]{1,0,2:T(8,128)(2,1)}, u32[]{:S(2)}) copy-start(bf16[64,64,64]{1,0,2:T(8,128)(2,1)} %reshape.403) | copy-start | bytes 1572868
  203.1 4.1 copy-start.11
  383.7 5.4 %copy-start.20 = (s32[64,1,1]{0,2,1:T(1,128)S(1)}, s32[64,1,1]{0,2,1:T(1,128)}, u32[]{:S(2)}) copy-start(s32[64,1,1]{0,2,1:T(1,128)} %get-tuple-element.5) | copy-start | bytes 772
  383.7 7.2 %copy-start.19 = (f32[64]{0:T(128)S(1)}, f32[64]{0:T(128)}, u32[]{:S(2)}) copy-start(f32[64]{0:T(128)} %copy-done.18) | copy-start | bytes 772
  383.7 7.2 %copy-start.26 = (s32[64]{0:T(128)S(1)}, s32[64]{0:T(128)}, u32[]{:S(2)}) copy-start(s32[64]{0:T(128)} %param.15) | copy-start | bytes 772
  385.1 19.3 %all-to-all-start.1 = ((bf16[8,10,4096]{2,1,0:T(8,128)(2,1)}), bf16[8,10,4096]{2,1,0:T(8,128)(2,1)S(1)}, u32[]{:S(2)}, u32[]{:S(2)}) async-start(bf16[8,10,4096]{2,1,0:T(8,128)(2,1)} %copy.78), calls=%async_computation.1 | async-start | bytes 2097152 | tf_op jit(solution)/shard_map/all_to_all | solution.py:14
  (12 other events, 24.3 us)
Sparse Core Ops, SparseCore 0:
  47.9 45.0 all-gather.1
  127.6 33.0 all-reduce.2
  214.4 154.6 all-reduce.4
where the time goes:
time: 422 us; the launch traced here: 415 us
  waiting for transfers between devices  246 us (58%)
  local copies, waits for them, and re-layouts  60.4 us (14%)
  matrix products  55.9 us (13%)
  other arithmetic  20.1 us (5%)
  between operations  14.7 us (3%)
  starting transfers between devices  9.43 us (2%)
  blocking collectives  8.24 us (2%)
    psum x1, waiting for transfers between devices, local(): d_full = lax.psum(d_normed, 'mp')  155 us
    all_gather x1, waiting for transfers between devices, local(): mixed = lax.all_gather(mixed_part, 'mp', axis=1, tiled=True)  31.9 us
    psum x1, waiting for transfers between devices, local(): pooled = lax.psum(pooled_branch, 'mp') + pooled_input  31.5 us
    all_to_all x2, waiting for transfers between devices, swap_rows(): return lax.all_to_all(buffer, 'dp', split_axis=0, concat_axis=0, tiled=True)  28.1 us
    scatter x2, local copies, waits for them, and re-layouts, local(): outgoing = jnp.zeros((n_data, capacity, row_len), jnp.bfloat16).at[target...  11.1 us
    scatter x2, local copies, waits for them, and re-layouts, local(): jnp.zeros((n_data, capacity, row_len), jnp.bfloat16).at[source, in_slot]  11.1 us
    all_to_all x2, starting transfers between devices, swap_rows(): return lax.all_to_all(buffer, 'dp', split_axis=0, concat_axis=0, tiled=True)  9.13 us
    another operation x6, local copies, waits for them, and re-layouts  8.6 us
  transfers between devices with their start and end apart: 5, of which 5 were waited for; matrix products, arithmetic and copies ran while one was open for 2% of the time, Pallas kernels for 0%

commit v1 on v0

--- a/solution.py
+++ b/solution.py
@@ -58,7 +58,13 @@
     own_lengths = lax.dynamic_slice_in_dim(lengths, device_index * sessions_dev, sessions_dev)
     len_mix = jnp.maximum(own_lengths, lengths[own_partner])
     qkv_full, out_full, up_full, down_full = (w_qkv, w_out, w_up, w_down)
-    mixed = lax.all_gather(mixed_part, "mp", axis=1, tiled=True)
+    size = lax.axis_size("mp")
+    held, pieces = (mixed_part, [mixed_part])
+    for _ in range(size - 1):
+        held = lax.ppermute(held, "mp", [(i, (i + 1) % size) for i in range(size)])
+        pieces.insert(0, held)
+    line = jnp.concatenate(pieces, axis=1)
+    mixed = jnp.roll(line, (lax.axis_index("mp") + 1) * mixed_part.shape[1], axis=1)
     layer_sessions = mixed.shape[0]
     events = mixed.shape[1]
     rows = layer_sessions * events

time: 422 us -> 419 us (level)
  waiting for transfers between devices: 246 us -> 241 us
    all_gather x1 -> x0, waiting for transfers between devices: 31.9 us -> none  [local(): mixed = lax.all_gather(mixed_part, 'mp', axis=1, tiled=True)]
    ppermute x0 -> x3, waiting for transfers between devices: none -> 24.9 us  [local(): held = lax.ppermute(held, 'mp', [(i, (i + 1) % size) for i in range(size)])]
  transfers between devices with their start and end apart: 5 -> 7, of which waited for: 5 -> 7; matrix products, arithmetic and copies ran while one was open for 2% -> 2% of each run, Pallas kernels for 0% -> 0%
where the time goes in v1:
time: 419 us; the launch traced here: 412 us
  waiting for transfers between devices  241 us (58%)
  local copies, waits for them, and re-layouts  63 us (15%)
  matrix products  54.9 us (13%)
  other arithmetic  18.9 us (5%)
  between operations  15.1 us (4%)
  starting transfers between devices  11 us (3%)
  blocking collectives  8.25 us (2%)
    psum x1, waiting for transfers between devices, local(): d_full = lax.psum(d_normed, 'mp')  155 us
    psum x1, waiting for transfers between devices, local(): pooled = lax.psum(pooled_branch, 'mp') + pooled_input  32.9 us
    all_to_all x2, waiting for transfers between devices, swap_rows(): return lax.all_to_all(buffer, 'dp', split_axis=0, concat_axis=0, tiled=True)  28.1 us
    ppermute x3, waiting for transfers between devices, local(): held = lax.ppermute(held, 'mp', [(i, (i + 1) % size) for i in range(size)])  24.9 us
    scatter x2, local copies, waits for them, and re-layouts, local(): outgoing = jnp.zeros((n_data, capacity, row_len), jnp.bfloat16).at[target...  11.1 us
    scatter x2, local copies, waits for them, and re-layouts, local(): jnp.zeros((n_data, capacity, row_len), jnp.bfloat16).at[source, in_slot]  11.1 us
    all_to_all x2, starting transfers between devices, swap_rows(): return lax.all_to_all(buffer, 'dp', split_axis=0, concat_axis=0, tiled=True)  9.13 us
    another operation x6, local copies, waits for them, and re-layouts  8.54 us
  transfers between devices with their start and end apart: 7, of which 7 were waited for; matrix products, arithmetic and copies ran while one was open for 2% of the time, Pallas kernels for 0%

profile of v1, /device:TPU:0, one launch (start us, length us, event | category | flops | bytes accessed | tf_op | source)
XLA Modules:
  0.0 411.7 jit_solution(18122296024606854064)
XLA Ops:
  12.3 9.7 %scatter_fusion = bf16[8,10,4096]{2,0,1:T(8,128)(2,1)S(1)} fusion(bf16[8,10,4096]{2,0,1:T(8,128)(2,1)S(1)} %broadcast.355.clone, s32[64]{0:T(128)S(1)} %get-tuple-element.15, bf16[64,4096]{1,0:T(8,128)(2,1)S(1)} %bitcast.215), kind=kCustom, calls=%fused_computation.8 | custom fusion | bytes 1573376 | tf_op jit(solution)/shard_map/scatter | solution.py:49
  23.4 5.2 %all-to-all-start = ((bf16[8,10,4096]{2,1,0:T(8,128)(2,1)}), bf16[8,10,4096]{2,1,0:T(8,128)(2,1)S(1)}, u32[]{:S(2)}, u32[]{:S(2)}) async-start(bf16[8,10,4096]{2,1,0:T(8,128)(2,1)} %copy.60), calls=%async_computation | async-start | bytes 2097152 | tf_op jit(solution)/shard_map/all_to_all | solution.py:14
  28.8 15.1 %all-to-all-done = bf16[8,10,4096]{2,1,0:T(8,128)(2,1)S(1)} async-done(((bf16[8,10,4096]{2,1,0:T(8,128)(2,1)}), bf16[8,10,4096]{2,1,0:T(8,128)(2,1)S(1)}, u32[]{:S(2)}, u32[]{:S(2)}) %all-to-all-start) | async-done | bytes 655392 | tf_op jit(solution)/shard_map/all_to_all | solution.py:14
  44.3 2.2 gather_fusion.2
  49.4 8.2 %all_gather.3 = bf16[512,128]{1,0:T(8,128)(2,1)S(1)} all-gather(bf16[64,128]{1,0:T(8,128)(2,1)S(1)} %copy-done.18), channel_id=1, replica_groups=mesh['dp'=8,'mp'=4] {'dp'}, dimensions={0}, use_global_device_ids=true | all-gather | bytes 147456 | tf_op jit(solution)/shard_map/all_gather | solution.py:23
  60.1 13.6 %collective-permute-done.1 = bf16[64,16,256]{2,1,0:T(8,128)(2,1)S(1)} collective-permute-done((bf16[64,16,256]{2,1,0:T(8,128)(2,1)S(1)}, bf16[64,16,256]{2,1,0:T(8,128)(2,1)S(1)}, u32[]{:S(2)}, u32[]{:S(2)}) %collective-permute-start.1) | collective-permute-done | bytes 524320 | tf_op jit(solution)/shard_map/ppermute | solution.py:64
  77.6 9.2 %collective-permute-done.2 = bf16[64,16,256]{2,1,0:T(8,128)(2,1)S(1)} collective-permute-done((bf16[64,16,256]{2,1,0:T(8,128)(2,1)S(1)}, bf16[64,16,256]{2,1,0:T(8,128)(2,1)S(1)}, u32[]{:S(2)}, u32[]{:S(2)}) %collective-permute-start.2) | collective-permute-done | bytes 524320 | tf_op jit(solution)/shard_map/ppermute | solution.py:64
  90.1 4.3 %broadcast_subtract_fusion = (f32[64,64,256]{2,1,0:T(8,128)}, f32[64,64]{1,0:T(8,128)S(1)}) fusion(f32[64,64]{1,0:T(8,128)S(1)} %broadcast_multiply_fusion.2, bf16[64,128,256]{2,1,0:T(8,128)(2,1)} %copy-done.3, s32[]{:T(128)S(6)} %select_n.129), kind=kLoop, calls=%fused_computation.45 | loop fusion | flops 4190208 | bytes 6324228 | tf_op jit(solution)/shard_map/sub | solution.py:76
  94.4 2.5 fusion.10
  104.7 3.7 fusion.135
  108.4 5.0 %fusion.26 = (f32[64,64]{1,0:T(8,128)S(1)}, f32[64,64,64]{1,2,0:T(8,128)S(1)}) fusion(f32[64,64]{1,0:T(8,128)S(1)} %copy-done.16, bf16[64,64,64]{1,0,2:T(8,128)(2,1)S(1)} %copy-done.8, bf16[64,64,64]{1,0,2:T(8,128)(2,1)S(1)} %copy-done.6), kind=kOutput, calls=%fused_computation.48 | convolution fusion | flops 34336768 | bytes 2129920 | tf_op jit(solution)/shard_map/sthc,srhc->shtr/dot_general | solution.py:90
  123.5 2.5 fusion.52
  126.0 32.9 %all-reduce.3.cloned.1.call-done = f32[64,256]{1,0:T(8,128)} async-done(((f32[64,256]{1,0:T(8,128)}), f32[64,256]{1,0:T(8,128)}) %all-reduce.3.cloned.1.call-update) | async-done | bytes 65552 | tf_op jit(solution)/shard_map/psum | solution.py:118
  164.5 2.8 reshape.407
  167.3 3.8 fusion.60
  171.1 3.4 fusion.45
  174.5 6.9 %fusion.49 = bf16[64,64,1,64]{1,3,0,2:T(8,128)(2,1)} fusion(f32[64,64,64]{1,2,0:T(8,128)} %fusion.60, bf16[64,64,64]{1,0,2:T(8,128)(2,1)} %reshape.404, f32[64,64,64]{1,2,0:T(8,128)} %copy-done.30, f32[64,64]{1,0:T(8,128)} %copy-done.32, f32[64,64]{1,0:T(8,128)} %fusion.82), kind=kOutput, calls=%fused_computation.64 | convolution fusion | flops 36704320 | bytes 3178496 | tf_op jit(solution)/shard_map/shtr,srhc->sthc/dot_general | solution.py:163
  181.3 7.5 %fusion.46 = bf16[64,64,1,64]{1,3,0,2:T(8,128)(2,1)} fusion(f32[64,64,64]{1,2,0:T(8,128)} %fusion.60, bf16[64,64,64]{1,0,2:T(8,128)(2,1)S(1)} %copy-done.7, f32[64,64,64]{1,2,0:T(8,128)} %copy-done.30, f32[64,64]{1,0:T(8,128)} %copy-done.32, f32[64,64]{1,0:T(8,128)} %fusion.82), kind=kOutput, calls=%fused_computation.63 | convolution fusion | flops 36704320 | bytes 3178496 | tf_op jit(solution)/shard_map/shtr,sthc->srhc/dot_general | solution.py:166
  199.4 4.1 %convolution_bitcast_fusion = f32[4096,256]{1,0:T(8,128)} fusion(bf16[3,256,64]{1,2,0:T(8,128)(2,1)} %param.17, bf16[1,4096,64]{1,2,0:T(8,128)(2,1)} %stack.14, bf16[1,4096,64]{1,2,0:T(8,128)(2,1)} %stack.13, bf16[1,4096,64]{1,2,0:T(8,128)(2,1)} %stack.12), kind=kOutput, calls=%fused_computation.14 | convolution fusion | flops 404226048 | bytes 5865472 | tf_op jit(solution)/shard_map/jrf,jdf->rd/dot_general | solution.py:170
  203.6 7.0 %convolution_add_fusion = f32[4096,256]{1,0:T(8,128)} fusion(f32[4096,256]{1,0:T(8,128)} %convolution_bitcast_fusion, bf16[256,256]{1,0:T(8,128)(2,1)S(1)} %copy-done.10, f32[4096,256]{1,0:T(8,128)} %fusion.135, bf16[4096,256]{1,0:T(8,128)(2,1)S(1)} %fusion.8, bf16[256,256]{1,0:T(8,128)(2,1)S(1)} %copy-done), kind=kOutput, calls=%fused_computation.13 | convolution fusion | flops 1095761920 | bytes 14942208 | tf_op jit(solution)/shard_map/rf,df->rd/dot_general | solution.py:172
  210.7 154.7 %all-reduce.5.cloned.1.call-done = f32[64,64,256]{2,1,0:T(8,128)} async-done(((f32[64,64,256]{2,1,0:T(8,128)}), f32[64,64,256]{2,1,0:T(8,128)}) %all-reduce.5.cloned.1.call-update) | async-done | bytes 4194320 | tf_op jit(solution)/shard_map/psum | solution.py:179
  370.3 9.7 %scatter_fusion.1 = bf16[8,10,4096]{2,0,1:T(8,128)(2,1)S(1)} fusion(bf16[8,10,4096]{2,0,1:T(8,128)(2,1)S(1)} %broadcast.355, s32[64]{0:T(128)S(1)} %get-tuple-element.16, bf16[64,4096]{1,0:T(8,128)(2,1)S(1)} %multiply_convert_fusion.3), kind=kCustom, calls=%fused_computation.9 | custom fusion | bytes 1573376 | tf_op jit(solution)/shard_map/scatter | solution.py:190
  381.4 3.9 all-to-all-start.1
  387.7 13.0 %all-to-all-done.1 = bf16[8,10,4096]{2,1,0:T(8,128)(2,1)S(1)} async-done(((bf16[8,10,4096]{2,1,0:T(8,128)(2,1)}), bf16[8,10,4096]{2,1,0:T(8,128)(2,1)S(1)}, u32[]{:S(2)}, u32[]{:S(2)}) %all-to-all-start.1) | async-done | bytes 655392 | tf_op jit(solution)/shard_map/all_to_all | solution.py:14
  (168 shorter events, 65.6 us)
Async XLA Ops:
  7.2 109.9 %copy-start = (bf16[256,256]{1,0:T(8,128)(2,1)S(1)}, bf16[256,256]{1,0:T(8,128)(2,1)}, u32[]{:S(2)}) copy-start(bf16[256,256]{1,0:T(8,128)(2,1)} %param.20) | copy-start | bytes 393220
  22.0 6.8 %copy-start.28 = (s32[64]{0:T(128)S(1)}, s32[64]{0:T(128)}, u32[]{:S(2)}) copy-start(s32[64]{0:T(128)} %param.15) | copy-start | bytes 772
  23.4 20.6 %all-to-all-start = ((bf16[8,10,4096]{2,1,0:T(8,128)(2,1)}), bf16[8,10,4096]{2,1,0:T(8,128)(2,1)S(1)}, u32[]{:S(2)}, u32[]{:S(2)}) async-start(bf16[8,10,4096]{2,1,0:T(8,128)(2,1)} %copy.60), calls=%async_computation | async-start | bytes 2097152 | tf_op jit(solution)/shard_map/all_to_all | solution.py:14
  28.6 130.4 %all-reduce.3.cloned.1.call-start = ((), (), s32[]{:S(2)}) async-start(), calls=%async_computation.2 | async-start | bytes 131072 | tf_op jit(solution)/shard_map/psum | solution.py:118
  28.8 17.9 %copy-start.22 = (f32[64]{0:T(128)}, f32[64]{0:T(128)S(1)}, u32[]{:S(2)}) copy-start(f32[64]{0:T(128)S(1)} %get-tuple-element.21) | copy-start | bytes 772
  28.8 17.9 %copy-start.25 = (f32[64]{0:T(128)}, f32[64]{0:T(128)S(1)}, u32[]{:S(2)}) copy-start(f32[64]{0:T(128)S(1)} %get-tuple-element.20) | copy-start | bytes 772
  47.0 12.8 %collective-permute-start = (bf16[64,16,256]{2,1,0:T(8,128)(2,1)S(1)}, bf16[64,16,256]{2,1,0:T(8,128)(2,1)S(1)}, u32[]{:S(2)}, u32[]{:S(2)}) collective-permute-start(bf16[64,16,256]{2,1,0:T(8,128)(2,1)S(1)} %fusion.57), channel_id=1, source_target_pairs={{0,1},{1,2},{2,3},{3,0},{4,5},{5,6},{6,7},{7,4},{8,9},{9,10},{10,1... | collective-permute-start | bytes 1572872 | tf_op jit(solution)/shard_map/ppermute | solution.py:64
  59.8 13.9 %collective-permute-start.1 = (bf16[64,16,256]{2,1,0:T(8,128)(2,1)S(1)}, bf16[64,16,256]{2,1,0:T(8,128)(2,1)S(1)}, u32[]{:S(2)}, u32[]{:S(2)}) collective-permute-start(bf16[64,16,256]{2,1,0:T(8,128)(2,1)S(1)} %collective-permute-done), channel_id=1, source_target_pairs={{0,1},{1,2},{2,3},{3,0},{4,5},{5,6},{6,7},{7,4},{8,9},{9,10},{10,1... | collective-permute-start | bytes 1572872 | tf_op jit(solution)/shard_map/ppermute | solution.py:64
  73.7 13.1 %collective-permute-start.2 = (bf16[64,16,256]{2,1,0:T(8,128)(2,1)S(1)}, bf16[64,16,256]{2,1,0:T(8,128)(2,1)S(1)}, u32[]{:S(2)}, u32[]{:S(2)}) collective-permute-start(bf16[64,16,256]{2,1,0:T(8,128)(2,1)S(1)} %collective-permute-done.1), channel_id=1, source_target_pairs={{0,1},{1,2},{2,3},{3,0},{4,5},{5,6},{6,7},{7,4},{8,9},{9,10},{10,1... | collective-permute-start | bytes 1572872 | tf_op jit(solution)/shard_map/ppermute | solution.py:64
  122.6 36.4 %copy-start.9 = (bf16[256,128]{1,0:T(8,128)(2,1)S(1)}, bf16[256,128]{1,0:T(8,128)(2,1)}, u32[]{:S(2)}) copy-start(bf16[256,128]{1,0:T(8,128)(2,1)} %param.21) | copy-start | bytes 196612
  122.6 38.1 %copy-start.14 = (f32[64,128]{1,0:T(8,128)S(1)}, f32[64,128]{1,0:T(8,128)}, u32[]{:S(2)}) copy-start(f32[64,128]{1,0:T(8,128)} %gather_fusion.4) | copy-start | bytes 98308
  122.6 38.1 %copy-start.15 = (f32[64,128]{1,0:T(8,128)S(1)}, f32[64,128]{1,0:T(8,128)}, u32[]{:S(2)}) copy-start(f32[64,128]{1,0:T(8,128)} %gather_fusion.3) | copy-start | bytes 98308
  122.6 38.1 %copy-start.23 = (f32[64]{0:T(128)S(1)}, f32[64]{0:T(128)}, u32[]{:S(2)}) copy-start(f32[64]{0:T(128)} %copy-done.22) | copy-start | bytes 772
  122.6 38.1 %copy-start.26 = (f32[64]{0:T(128)S(1)}, f32[64]{0:T(128)}, u32[]{:S(2)}) copy-start(f32[64]{0:T(128)} %copy-done.25) | copy-start | bytes 772
  123.3 242.1 %all-reduce.5.cloned.1.call-start = ((), (), s32[]{:S(2)}) async-start(), calls=%async_computation.3 | async-start | bytes 8388608 | tf_op jit(solution)/shard_map/psum | solution.py:179
  159.0 4.0 copy-start.12
  167.3 3.8 copy-start.31
  167.3 3.8 copy-start.33
  174.5 6.9 %copy-start.7 = (bf16[64,64,64]{1,0,2:T(8,128)(2,1)S(1)}, bf16[64,64,64]{1,0,2:T(8,128)(2,1)}, u32[]{:S(2)}) copy-start(bf16[64,64,64]{1,0,2:T(8,128)(2,1)} %reshape.403) | copy-start | bytes 1572868
  199.4 4.1 %copy-start.10 = (bf16[256,256]{1,0:T(8,128)(2,1)S(1)}, bf16[256,256]{1,0:T(8,128)(2,1)}, u32[]{:S(2)}) copy-start(bf16[256,256]{1,0:T(8,128)(2,1)} %param.19) | copy-start | bytes 393220
  380.0 5.4 %copy-start.21 = (s32[64,1,1]{0,2,1:T(1,128)S(1)}, s32[64,1,1]{0,2,1:T(1,128)}, u32[]{:S(2)}) copy-start(s32[64,1,1]{0,2,1:T(1,128)} %get-tuple-element.5) | copy-start | bytes 772
  380.0 7.2 %copy-start.20 = (f32[64]{0:T(128)S(1)}, f32[64]{0:T(128)}, u32[]{:S(2)}) copy-start(f32[64]{0:T(128)} %copy-done.19) | copy-start | bytes 772
  380.0 7.2 %copy-start.29 = (s32[64]{0:T(128)S(1)}, s32[64]{0:T(128)}, u32[]{:S(2)}) copy-start(s32[64]{0:T(128)} %param.15) | copy-start | bytes 772
  381.4 19.3 %all-to-all-start.1 = ((bf16[8,10,4096]{2,1,0:T(8,128)(2,1)}), bf16[8,10,4096]{2,1,0:T(8,128)(2,1)S(1)}, u32[]{:S(2)}, u32[]{:S(2)}) async-start(bf16[8,10,4096]{2,1,0:T(8,128)(2,1)} %copy.78), calls=%async_computation.1 | async-start | bytes 2097152 | tf_op jit(solution)/shard_map/all_to_all | solution.py:14
  (17 other events, 42.7 us)
Sparse Core Ops, SparseCore 0:
  123.4 35.5 all-reduce.2
  210.7 154.6 all-reduce.4
